TPU v7x, 32 devices: a whole 2x2x4 slice. The times are simulated.
32 devices in a mesh: row: 4 (over y, core), col: 8 (over z, x).
Axes of the slice: x: 2, y: 2, z: 4, core: 2. Of those that a mesh axis runs over, the one named last changes fastest.
Arguments:
- pixels: bfloat16 [128, 256, 588], P('row', 'col'), may hold values from -6 to 6
- text: bfloat16 [12288, 1024], P(('row', 'col')), may hold values from -6 to 6
- token_source: int32 [36864], P(('row', 'col')), may hold values from 0 to 1407, as said below
- example_ids: int32 [36864], P(('row', 'col')), may hold values from 0 to 95, as said below
- cotangent: bfloat16 [36864, 1024], P(('row', 'col')), may hold values from -6 to 6
- conv_weight: bfloat16 [588, 1664], P(None, ('row', 'col')), may hold values from -0.25 to 0.25
- conv_bias: bfloat16 [1664], P(('row', 'col')), may hold values from -3 to 3
- proj_weight: bfloat16 [1664, 1024], P(None, ('row', 'col')), may hold values from -0.15625 to 0.15625
- proj_bias: bfloat16 [1024], P(('row', 'col')), may hold values from -3 to 3
- first_gain: bfloat16 [1024], P(('row', 'col')), may hold values from 0.099609375 to 1.8984375
- query_weight: bfloat16 [1024, 1024], P(('row', 'col')), may hold values from -0.1875 to 0.1875
- key_weight: bfloat16 [1024, 1024], P(('row', 'col')), may hold values from -0.1875 to 0.1875
- value_weight: bfloat16 [1024, 1024], P(('row', 'col')), may hold values from -0.1875 to 0.1875
- out_weight: bfloat16 [1024, 1024], P(None, ('row', 'col')), may hold values from -3 to 3
- second_gain: bfloat16 [1024], P(('row', 'col')), may hold values from 0.099609375 to 1.8984375
- gate_weight: bfloat16 [1024, 2816], P(('row', 'col')), may hold values from -0.1875 to 0.1875
- up_weight: bfloat16 [1024, 2816], P(('row', 'col')), may hold values from -0.1875 to 0.1875
- down_weight: bfloat16 [2816, 1024], P(None, ('row', 'col')), may hold values from -0.109375 to 0.109375
Outputs:
- output: bfloat16 [36864, 1024], P(('row', 'col'))
- pixel_grad: float32 [128, 256, 588], P('row', 'col')
- conv_weight_grad: float32 [588, 1664], P(None, ('row', 'col'))
- conv_bias_grad: float32 [1664], P(('row', 'col'))
- proj_weight_grad: float32 [1664, 1024], P(None, ('row', 'col'))
- proj_bias_grad: float32 [1024], P(('row', 'col'))
- first_gain_grad: float32 [1024], P(('row', 'col'))
- query_grad: float32 [1024, 1024], P(('row', 'col'))
- key_grad: float32 [1024, 1024], P(('row', 'col'))
- value_grad: float32 [1024, 1024], P(('row', 'col'))
- out_grad: float32 [1024, 1024], P(None, ('row', 'col'))
- second_gain_grad: float32 [1024], P(('row', 'col'))
- gate_grad: float32 [1024, 2816], P(('row', 'col'))
- up_grad: float32 [1024, 2816], P(('row', 'col'))
- down_grad: float32 [2816, 1024], P(None, ('row', 'col'))
Inputs may be any that keep to these rules, and one draw needn't show every extreme that they name: `token_source`: within each packed row (tokens t with the same t div 1152) the sources are distinct; a row takes either all 1024 patch slots and text slots 1024 to 1151, or three quarters of its patch slots and all 384 text slots; slots that no token names are empty. `example_ids`: A packed row holds one example of 1152 tokens or three of 384 tokens each, every example contiguous and within one row; ids of different examples differ.
All inputs are finite; a program needn't handle non-finite values.
Results may differ from a plain program's by a relative error of at most 0.015.
Values may be sent and summed in bfloat16 or wider, within the bound.
No kernel may reach another device: no remote copies, remote signals or barrier semaphores. Data moves between devices by JAX's collectives and lax.ppermute only.
A program may use at most 256 MiB of HBM per device.

v0:
```python
import jax
import jax.numpy as jnp
from jax import lax
from jax.sharding import PartitionSpec as P

D = 1024
H = 16
HD = 64
PATCH_SLOTS = 1024
TEXT = 128
ROW = 1152


def normed(values, gain):
    return values * lax.rsqrt(jnp.mean(values * values, axis=-1, keepdims=True) + 1e-06) * gain


def gelu_tanh(values):
    return jax.nn.gelu(values, approximate=True)


def matmul(left, right):
    return jnp.dot(left, right, preferred_element_type=jnp.float32)


def left_contract(left, right):
    return lax.dot_general(
        left, right, (((0,), (0,)), ((), ())), preferred_element_type=jnp.float32
    )


def right_contract(left, right):
    return lax.dot_general(
        left, right, (((1,), (1,)), ((), ())), preferred_element_type=jnp.float32
    )


def split_heads(values):
    return values.reshape(values.shape[0], H, HD).transpose(1, 0, 2)


def merge_heads(values):
    return values.transpose(1, 0, 2).reshape(values.shape[1], H * HD)


def masked_scores(query, keys, same_example):
    return jnp.where(same_example, right_contract(query, keys) * 0.125, -1000000000.0)


def attend_row(parts):
    queries, keys_all, values_all, example_row = parts
    same_example = example_row[:, None] == example_row[None, :]

    def one_head(pieces):
        query, keys, values = pieces
        scores = masked_scores(query, keys, same_example)
        row_max = jnp.max(scores, axis=-1, keepdims=True)
        powers = jnp.exp(scores - row_max)
        totals = jnp.sum(powers, axis=-1, keepdims=True)
        chances = (powers / totals).astype(jnp.bfloat16)
        return (matmul(chances, values), (row_max + jnp.log(totals))[:, 0])

    outputs, logsum = lax.map(
        one_head, (split_heads(queries), split_heads(keys_all), split_heads(values_all))
    )
    return (merge_heads(outputs), logsum)


def attend_back(parts):
    queries, keys_all, values_all, grads_all, logsum, example_row = parts
    same_example = example_row[:, None] == example_row[None, :]

    def one_head(pieces):
        query, keys, values, grads, logs = pieces
        scores = masked_scores(query, keys, same_example)
        chances = jnp.exp(scores - logs[:, None])
        grad_chances = right_contract(grads, values)
        deltas = jnp.sum(chances * grad_chances, axis=-1, keepdims=True)
        grad_scores = (chances * (grad_chances - deltas)).astype(jnp.bfloat16)
        return (
            matmul(grad_scores, keys) * 0.125,
            left_contract(grad_scores, query) * 0.125,
            left_contract(chances.astype(jnp.bfloat16), grads),
        )

    grad_query, grad_keys, grad_values = lax.map(
        one_head,
        (
            split_heads(queries),
            split_heads(keys_all),
            split_heads(values_all),
            split_heads(grads_all),
            logsum,
        ),
    )
    return (merge_heads(grad_query), merge_heads(grad_keys), merge_heads(grad_values))


def shards(
    pixels,
    text,
    token_source,
    example_ids,
    cotangent,
    conv_weight,
    conv_bias,
    proj_weight,
    proj_bias,
    first_gain,
    query_weight,
    key_weight,
    value_weight,
    out_weight,
    second_gain,
    gate_weight,
    up_weight,
    down_weight,
):
    (
        conv_whole,
        conv_add,
        proj_whole,
        proj_add,
        gain_one,
        query_whole,
        key_whole,
        value_whole,
        out_whole,
        gain_two,
    ) = (
        lax.all_gather(conv_weight, ("row", "col"), axis=1, tiled=True),
        lax.all_gather(conv_bias, ("row", "col"), axis=0, tiled=True),
        lax.all_gather(proj_weight, ("row", "col"), axis=1, tiled=True),
        lax.all_gather(proj_bias, ("row", "col"), axis=0, tiled=True),
        lax.all_gather(first_gain, ("row", "col"), axis=0, tiled=True),
        lax.all_gather(query_weight, ("row", "col"), axis=0, tiled=True),
        lax.all_gather(key_weight, ("row", "col"), axis=0, tiled=True),
        lax.all_gather(value_weight, ("row", "col"), axis=0, tiled=True),
        lax.all_gather(out_weight, ("row", "col"), axis=1, tiled=True),
        lax.all_gather(second_gain, ("row", "col"), axis=0, tiled=True),
    )
    gate_whole, up_whole, down_whole = (
        lax.all_gather(gate_weight, ("row", "col"), axis=0, tiled=True),
        lax.all_gather(up_weight, ("row", "col"), axis=0, tiled=True),
        lax.all_gather(down_weight, ("row", "col"), axis=1, tiled=True),
    )
    patch_rows = pixels.reshape(-1, pixels.shape[-1])
    visual = (matmul(patch_rows, conv_whole) + conv_add.astype(jnp.float32)).astype(jnp.bfloat16)
    embedded = (matmul(visual, proj_whole) + proj_add.astype(jnp.float32)).astype(jnp.bfloat16)
    arrived = lax.all_to_all(embedded, ("row", "col"), split_axis=0, concat_axis=0, tiled=True)
    row_total = token_source.shape[0] // ROW
    pooled = jnp.concatenate(
        (arrived.reshape(row_total, PATCH_SLOTS, D), text.reshape(row_total, 3 * TEXT, D)), axis=1
    )
    sources = token_source.reshape(row_total, ROW)
    example_rows = example_ids.reshape(row_total, ROW)
    residual = (
        jax.vmap(lambda pooled_row, chosen: pooled_row[chosen])(pooled, sources)
        .reshape(-1, D)
        .astype(jnp.float32)
    )

    def by_rows(values):
        return values.reshape(row_total, ROW, values.shape[-1])

    gain_first = gain_one.astype(jnp.float32)
    gain_second = gain_two.astype(jnp.float32)
    normal_in = normed(residual, gain_first).astype(jnp.bfloat16)
    queries = matmul(normal_in, query_whole).astype(jnp.bfloat16)
    keys_all = matmul(normal_in, key_whole).astype(jnp.bfloat16)
    values_all = matmul(normal_in, value_whole).astype(jnp.bfloat16)
    attended, logsum = lax.map(
        attend_row, (by_rows(queries), by_rows(keys_all), by_rows(values_all), example_rows)
    )
    mixed = attended.reshape(-1, D).astype(jnp.bfloat16)
    middle = residual + matmul(mixed, out_whole)
    normal_mid = normed(middle, gain_second).astype(jnp.bfloat16)
    gate = matmul(normal_mid, gate_whole)
    upward = matmul(normal_mid, up_whole)
    gate_act = gelu_tanh(gate)
    hidden = (gate_act * upward).astype(jnp.bfloat16)
    output = (middle + matmul(hidden, down_whole)).astype(jnp.bfloat16)
    gate_whole, up_whole, down_whole = (
        lax.all_gather(gate_weight, ("row", "col"), axis=0, tiled=True),
        lax.all_gather(up_weight, ("row", "col"), axis=0, tiled=True),
        lax.all_gather(down_weight, ("row", "col"), axis=1, tiled=True),
    )
    grad_down = left_contract(hidden, cotangent)
    grad_hidden = right_contract(cotangent, down_whole)
    gelu_pull = jax.vjp(gelu_tanh, gate)[1]
    grad_gate = gelu_pull(grad_hidden * upward)[0].astype(jnp.bfloat16)
    grad_upward = (grad_hidden * gate_act).astype(jnp.bfloat16)
    ffn_sums = (
        lax.psum_scatter(
            left_contract(normal_mid, grad_gate), ("row", "col"), scatter_dimension=0, tiled=True
        ),
        lax.psum_scatter(
            left_contract(normal_mid, grad_upward), ("row", "col"), scatter_dimension=0, tiled=True
        ),
        lax.psum_scatter(grad_down, ("row", "col"), scatter_dimension=1, tiled=True),
    )
    grad_normal_mid = right_contract(grad_gate, gate_whole) + right_contract(grad_upward, up_whole)
    grad_middle_norm, grad_gain_two = jax.vjp(normed, middle, gain_second)[1](grad_normal_mid)
    grad_middle = cotangent.astype(jnp.float32) + grad_middle_norm
    grad_branch = grad_middle.astype(jnp.bfloat16)
    (
        conv_whole,
        conv_add,
        proj_whole,
        proj_add,
        gain_one,
        query_whole,
        key_whole,
        value_whole,
        out_whole,
        gain_two,
    ) = (
        lax.all_gather(conv_weight, ("row", "col"), axis=1, tiled=True),
        lax.all_gather(conv_bias, ("row", "col"), axis=0, tiled=True),
        lax.all_gather(proj_weight, ("row", "col"), axis=1, tiled=True),
        lax.all_gather(proj_bias, ("row", "col"), axis=0, tiled=True),
        lax.all_gather(first_gain, ("row", "col"), axis=0, tiled=True),
        lax.all_gather(query_weight, ("row", "col"), axis=0, tiled=True),
        lax.all_gather(key_weight, ("row", "col"), axis=0, tiled=True),
        lax.all_gather(value_weight, ("row", "col"), axis=0, tiled=True),
        lax.all_gather(out_weight, ("row", "col"), axis=1, tiled=True),
        lax.all_gather(second_gain, ("row", "col"), axis=0, tiled=True),
    )
    grad_out = left_contract(mixed, grad_branch)
    grad_mixed = right_contract(grad_branch, out_whole).astype(jnp.bfloat16)
    grad_query, grad_keys, grad_values = lax.map(
        attend_back,
        (
            by_rows(queries),
            by_rows(keys_all),
            by_rows(values_all),
            by_rows(grad_mixed),
            logsum,
            example_rows,
        ),
    )
    grad_query = grad_query.reshape(-1, D).astype(jnp.bfloat16)
    grad_keys = grad_keys.reshape(-1, D).astype(jnp.bfloat16)
    grad_values = grad_values.reshape(-1, D).astype(jnp.bfloat16)
    grad_normal_in = (
        right_contract(grad_query, query_whole)
        + right_contract(grad_keys, key_whole)
        + right_contract(grad_values, value_whole)
    )
    grad_res_norm, grad_gain_one = jax.vjp(normed, residual, gain_first)[1](grad_normal_in)
    grad_residual = grad_middle + grad_res_norm
    pool_width = PATCH_SLOTS + 3 * TEXT
    grad_pooled = jax.vmap(
        lambda chosen, grads: jnp.zeros((pool_width, D), jnp.float32).at[chosen].add(grads)
    )(sources, by_rows(grad_residual))
    grad_arrived = grad_pooled[:, :PATCH_SLOTS].reshape(-1, D).astype(jnp.bfloat16)
    grad_embedded = lax.all_to_all(
        grad_arrived, ("row", "col"), split_axis=0, concat_axis=0, tiled=True
    )
    grad_proj = left_contract(visual, grad_embedded)
    grad_proj_add = jnp.sum(grad_embedded.astype(jnp.float32), axis=0)
    grad_visual = right_contract(grad_embedded, proj_whole).astype(jnp.bfloat16)
    grad_conv = left_contract(patch_rows, grad_visual)
    grad_conv_add = jnp.sum(grad_visual.astype(jnp.float32), axis=0)
    grad_pixels = right_contract(grad_visual, conv_whole).reshape(pixels.shape)
    front_sums = (
        lax.psum_scatter(grad_conv, ("row", "col"), scatter_dimension=1, tiled=True),
        lax.psum_scatter(grad_conv_add, ("row", "col"), scatter_dimension=0, tiled=True),
        lax.psum_scatter(grad_proj, ("row", "col"), scatter_dimension=1, tiled=True),
        lax.psum_scatter(grad_proj_add, ("row", "col"), scatter_dimension=0, tiled=True),
        lax.psum_scatter(grad_gain_one, ("row", "col"), scatter_dimension=0, tiled=True),
        lax.psum_scatter(
            left_contract(normal_in, grad_query), ("row", "col"), scatter_dimension=0, tiled=True
        ),
        lax.psum_scatter(
            left_contract(normal_in, grad_keys), ("row", "col"), scatter_dimension=0, tiled=True
        ),
        lax.psum_scatter(
            left_contract(normal_in, grad_values), ("row", "col"), scatter_dimension=0, tiled=True
        ),
        lax.psum_scatter(grad_out, ("row", "col"), scatter_dimension=1, tiled=True),
        lax.psum_scatter(grad_gain_two, ("row", "col"), scatter_dimension=0, tiled=True),
    )
    return (
        output,
        grad_pixels,
        front_sums[0],
        front_sums[1],
        front_sums[2],
        front_sums[3],
        front_sums[4],
        front_sums[5],
        front_sums[6],
        front_sums[7],
        front_sums[8],
        front_sums[9],
        ffn_sums[0],
        ffn_sums[1],
        ffn_sums[2],
    )


def solution(mesh):
    return jax.shard_map(
        shards,
        mesh=mesh,
        in_specs=(
            P("row", "col", None),
            P(("row", "col"), None),
            P(("row", "col")),
            P(("row", "col")),
            P(("row", "col"), None),
            P(None, ("row", "col")),
            P(("row", "col")),
            P(None, ("row", "col")),
            P(("row", "col")),
            P(("row", "col")),
            P(("row", "col"), None),
            P(("row", "col"), None),
            P(("row", "col"), None),
            P(None, ("row", "col")),
            P(("row", "col")),
            P(("row", "col"), None),
            P(("row", "col"), None),
            P(None, ("row", "col")),
        ),
        out_specs=(
            P(("row", "col"), None),
            P("row", "col", None),
            P(None, ("row", "col")),
            P(("row", "col")),
            P(None, ("row", "col")),
            P(("row", "col")),
            P(("row", "col")),
            P(("row", "col"), None),
            P(("row", "col"), None),
            P(("row", "col"), None),
            P(None, ("row", "col")),
            P(("row", "col")),
            P(("row", "col"), None),
            P(("row", "col"), None),
            P(None, ("row", "col")),
        ),
        check_vma=False,
    )
```

profile of v0, /device:TPU:0, one launch (start us, length us, event | category | flops | bytes accessed | tf_op | source)
XLA Modules:
  0.0 2604.0 jit_solution(6728988985074785193)
XLA Ops:
  16.0 42.4 %all-reduce.10 = (bf16[1024]{0:T(1024)(128)(2,1)S(1)}, bf16[1664]{0:T(1024)(128)(2,1)S(1)}, bf16[1024]{0:T(1024)(128)(2,1)S(1)}, bf16[1024]{0:T(1024)(128)(2,1)S(1)}) all-reduce(bf16[1024]{0:T(1024)(128)(2,1)S(1)} %dynamic-update-slice.1, bf16[1664]{0:T(1024)(128)(2,1)S(1)} %dynamic-update-slice, ...), channel_id=1, replica_groups=mesh['row'=4,'col'=8] {'row','col'}, use_global_device_ids=true, to_apply=%add.1 | all-reduce | flops 4736 | bytes 18944
  58.4 12.4 all-gather.27.cloned.1.call-done
  78.0 54.7 %all-gather.11.cloned.1.call-done = bf16[1664,1024]{0,1:T(8,128)(2,1)} async-done(((bf16[1664,32]{0,1:T(8,128)(2,1)}), bf16[1664,1024]{0,1:T(8,128)(2,1)}) %all-gather.11.cloned.1.call-update) | async-done | bytes 3407888 | tf_op jit(solution)/shard_map/all_gather | solution.py:133
  132.7 8.3 add_convert_fusion.2
  150.5 53.3 %all-to-all-done = bf16[32,32,1024]{2,1,0:T(8,128)(2,1)S(1)} async-done(((bf16[32,32,1024]{2,1,0:T(8,128)(2,1)}), bf16[32,32,1024]{2,1,0:T(8,128)(2,1)S(1)}, u32[]{:S(2)}, u32[]{:S(2)}) %all-to-all-start) | async-done | bytes 2097184 | tf_op jit(solution)/shard_map/all_to_all | solution.py:150
  206.9 21.5 gather_fusion
  247.8 8.9 all-gather.15.cloned.1.call-done
  269.6 45.2 %all-gather.13.cloned.1.call-done = bf16[1024,1024]{1,0:T(8,128)(2,1)} async-done(((bf16[32,1024]{1,0:T(8,128)(2,1)}), bf16[1024,1024]{1,0:T(8,128)(2,1)}) %all-gather.13.cloned.1.call-update) | async-done | bytes 2097168 | tf_op jit(solution)/shard_map/all_gather | solution.py:136
  329.0 151.9 %while.48 = (s32[]{:T(128)}, bf16[16,1152,64]{1,2,0:T(8,128)(2,1)}, f32[16,1152]{1,0:T(8,128)S(1)}, bf16[16,1152,64]{2,1,0:T(8,128)(2,1)}, bf16[16,1152,64]{2,1,...) while((s32[]{:T(128)}, bf16[16,1152,64]{1,2,0:T(8,128)(2,1)}, ...), condition=%wide.region_4.5_spmd.clone, body=%wide.region_1.4_spmd.clone.sunk | while | flops 351681408 | bytes 38412412 | solution.py:63
  490.9 13.3 fusion.89
  511.0 13.0 fusion.90
  524.0 55.9 %all-gather.25.cloned.1.call-done = bf16[2816,1024]{0,1:T(8,128)(2,1)} async-done(((bf16[2816,32]{0,1:T(8,128)(2,1)}), bf16[2816,1024]{0,1:T(8,128)(2,1)}) %all-gather.25.cloned.1.call-update) | async-done | bytes 5767184 | tf_op jit(solution)/shard_map/all_gather | solution.py:145
  579.9 25.6 multiply_convert_fusion.1
  605.5 13.3 fusion.91
  618.9 11.6 multiply_reduce_fusion.1
  649.6 209.3 %while.49 = (s32[]{:T(128)}, bf16[16,1152,64]{1,2,0:T(8,128)(2,1)}, bf16[16,1152,64]{1,2,0:T(8,128)(2,1)}, bf16[16,1152,64]{1,2,0:T(8,128)(2,1)}, bf16[16,1152,6...) while((s32[]{:T(128)}, bf16[16,1152,64]{1,2,0:T(8,128)(2,1)}, ...), condition=%wide.region_9.10_spmd.clone, body=%wide.region_7.9_spmd.clone.sunk | while | flops 862763904 | bytes 42810480 | solution.py:86
  881.4 17.6 scatter_custom_fusion
  902.2 53.0 %all_to_all.18 = bf16[32,32,1024]{2,1,0:T(8,128)(2,1)S(1)} all-to-all(bf16[32,32,1024]{2,1,0:T(8,128)(2,1)S(1)} %bitcast.178), channel_id=1, replica_groups=mesh['row'=4,'col'=8] {'row','col'}, dimensions={0} | all-to-all | bytes 4194304 | tf_op jit(solution)/shard_map/all_to_all | solution.py:257
  996.2 8.0 fusion.93
  1004.3 13.6 fusion.94
  1018.4 13.5 fusion.95
  1031.9 13.7 fusion.96
  1045.7 13.3 add_convert_fusion.1
  1063.7 38.9 %all-reduce.9 = (f32[1664]{0:T(1024)S(1)}, f32[1024]{0:T(1024)S(1)}, f32[1024]{0:T(1024)S(1)}, f32[1024]{0:T(1024)S(1)}) all-reduce(f32[1664]{0:T(1024)S(1)} %get-tuple-element.307, f32[1024]{0:T(1024)S(1)} %convert_reduce_fusion.1, f32[1024]{0:T(1024)S(1)} %get-tuple-element.250, ...), channel_id=3, replica_groups=mesh['row'=4,'col'=8] {'row','col'}, use_global_device_ids=true, to_apply=%region_14.15.clone | all-reduce | flops 4736 | bytes 37888
  1114.1 138.6 %reduce-scatter.12.cloned.1.call-done = f32[32,1024]{1,0:T(8,128)} async-done(((f32[1024,1024]{1,0:T(8,128)}), f32[32,1024]{1,0:T(8,128)}) %reduce-scatter.12.cloned.1.call-update) | async-done | bytes 131088 | tf_op jit(solution)/shard_map/reduce_scatter | solution.py:272
  1252.7 145.2 %reduce-scatter.14.cloned.1.call-done = f32[32,1024]{1,0:T(8,128)} async-done(((f32[1024,1024]{1,0:T(8,128)}), f32[32,1024]{1,0:T(8,128)}) %reduce-scatter.14.cloned.1.call-update) | async-done | bytes 131088 | tf_op jit(solution)/shard_map/reduce_scatter | solution.py:275
  1397.9 144.6 %reduce-scatter.16.cloned.1.call-done = f32[32,1024]{1,0:T(8,128)} async-done(((f32[1024,1024]{1,0:T(8,128)}), f32[32,1024]{1,0:T(8,128)}) %reduce-scatter.16.cloned.1.call-update) | async-done | bytes 131088 | tf_op jit(solution)/shard_map/reduce_scatter | solution.py:278
  1542.5 145.0 %reduce-scatter.18.cloned.1.call-done = f32[1024,32]{0,1:T(8,128)} async-done(((f32[1024,1024]{0,1:T(8,128)}), f32[1024,32]{0,1:T(8,128)}) %reduce-scatter.18.cloned.1.call-update) | async-done | bytes 131088 | tf_op jit(solution)/shard_map/reduce_scatter | solution.py:281
  1687.5 155.7 %reduce-scatter.10.cloned.1.call-done = f32[1664,32]{0,1:T(8,128)} async-done(((f32[1664,1024]{0,1:T(8,128)}), f32[1664,32]{0,1:T(8,128)}) %reduce-scatter.10.cloned.1.call-update) | async-done | bytes 213008 | tf_op jit(solution)/shard_map/reduce_scatter | solution.py:269
  1843.2 251.7 %reduce-scatter.20.cloned.1.call-done = f32[32,2816]{1,0:T(8,128)} async-done(((f32[1024,2816]{1,0:T(8,128)}), f32[32,2816]{1,0:T(8,128)}) %reduce-scatter.20.cloned.1.call-update) | async-done | bytes 360464 | tf_op jit(solution)/shard_map/reduce_scatter | solution.py:194
  2095.0 250.7 %reduce-scatter.22.cloned.1.call-done = f32[32,2816]{1,0:T(8,128)} async-done(((f32[1024,2816]{1,0:T(8,128)}), f32[32,2816]{1,0:T(8,128)}) %reduce-scatter.22.cloned.1.call-update) | async-done | bytes 360464 | tf_op jit(solution)/shard_map/reduce_scatter | solution.py:197
  2345.7 251.2 %reduce-scatter.24.cloned.1.call-done = f32[2816,32]{0,1:T(8,128)} async-done(((f32[2816,1024]{0,1:T(8,128)}), f32[2816,32]{0,1:T(8,128)}) %reduce-scatter.24.cloned.1.call-update) | async-done | bytes 360464 | tf_op jit(solution)/shard_map/reduce_scatter | solution.py:200
  (405 shorter events, 553.9 us)
Async XLA Ops:
  7.2 66.4 %copy-start = (bf16[32,32,588]{2,1,0:T(8,128)(2,1)S(1)}, bf16[32,32,588]{2,1,0:T(8,128)(2,1)}, u32[]{:S(2)}) copy-start(bf16[32,32,588]{2,1,0:T(8,128)(2,1)} %param.22) | copy-start | bytes 3612676
  7.2 63.6 %all-gather.27.cloned.1.call-start = ((), (), s32[]{:S(2)}) async-start(), calls=%async_computation.26 | async-start | bytes 2365440 | tf_op jit(solution)/shard_map/all_gather | solution.py:131
  7.9 124.8 %all-gather.11.cloned.1.call-start = ((), (), s32[]{:S(2)}) async-start(), calls=%async_computation.10 | async-start | bytes 3514368 | tf_op jit(solution)/shard_map/all_gather | solution.py:133
  8.7 226.7 %all-gather.17.cloned.1.call-start = ((), (), s32[]{:S(2)}) async-start(), calls=%async_computation.13 | async-start | bytes 2162688 | tf_op jit(solution)/shard_map/all_gather | solution.py:138
  9.4 247.3 %all-gather.15.cloned.1.call-start = ((), (), s32[]{:S(2)}) async-start(), calls=%async_computation.12 | async-start | bytes 2162688 | tf_op jit(solution)/shard_map/all_gather | solution.py:137
  10.0 304.9 %all-gather.13.cloned.1.call-start = ((), (), s32[]{:S(2)}) async-start(), calls=%async_computation.11 | async-start | bytes 2162688 | tf_op jit(solution)/shard_map/all_gather | solution.py:136
  10.6 470.3 %all-gather.19.cloned.1.call-start = ((), (), s32[]{:S(2)}) async-start(), calls=%async_computation.14 | async-start | bytes 2162688 | tf_op jit(solution)/shard_map/all_gather | solution.py:139
  11.2 479.7 %all-gather.21.cloned.1.call-start = ((), (), s32[]{:S(2)}) async-start(), calls=%async_computation.15 | async-start | bytes 5947392 | tf_op jit(solution)/shard_map/all_gather | solution.py:143
  11.9 499.1 %all-gather.23.cloned.1.call-start = ((), (), s32[]{:S(2)}) async-start(), calls=%async_computation.16 | async-start | bytes 5947392 | tf_op jit(solution)/shard_map/all_gather | solution.py:144
  78.0 67.2 %copy-start.15 = (s32[1152]{0:T(1024)S(1)}, s32[1152]{0:T(1024)}, u32[]{:S(2)}) copy-start(s32[1152]{0:T(1024)} %param.24) | copy-start | bytes 13828
  141.0 8.7 copy-start.18
  141.0 8.7 copy-start.17
  141.0 62.8 %all-to-all-start = ((bf16[32,32,1024]{2,1,0:T(8,128)(2,1)}), bf16[32,32,1024]{2,1,0:T(8,128)(2,1)S(1)}, u32[]{:S(2)}, u32[]{:S(2)}) async-start(bf16[32,32,1024]{2,1,0:T(8,128)(2,1)} %bitcast.191), calls=%async_computation | async-start | bytes 4194304 | tf_op jit(solution)/shard_map/all_to_all | solution.py:150
  144.2 435.7 %all-gather.25.cloned.1.call-start = ((), (), s32[]{:S(2)}) async-start(), calls=%async_computation.17 | async-start | bytes 5947392 | tf_op jit(solution)/shard_map/all_gather | solution.py:145
  144.9 967.1 %all-reduce.13.cloned.1.call-start = ((), (), s32[]{:S(2)}) async-start(), calls=%async_computation.27 | async-start | bytes 7880704
  145.3 169.5 %copy-start.13 = (f32[1024]{0:T(1024)}, f32[1024]{0:T(1024)S(1)}, u32[]{:S(2)}) copy-start(f32[1024]{0:T(1024)S(1)} %convert_element_type.168) | copy-start | bytes 12292
  235.4 79.4 %copy-start.11 = (f32[1152]{0:T(1024)}, f32[1152]{0:T(1024)S(1)}, u32[]{:S(2)}) copy-start(f32[1152]{0:T(1024)S(1)} %fusion.73) | copy-start | bytes 13828
  321.7 7.3 copy-start.8
  605.5 13.3 copy-start.19
  605.5 13.3 copy-start.26
  618.9 11.7 copy-start.5
  649.6 209.3 %copy-start.22 = (bf16[1024,1024]{1,0:T(8,128)(2,1)S(1)}, bf16[1024,1024]{1,0:T(8,128)(2,1)}, u32[]{:S(2)}) copy-start(bf16[1024,1024]{1,0:T(8,128)(2,1)} %all-gather.15.cloned.1.call-done) | copy-start | bytes 6291460
  863.7 8.3 slice-start
  902.0 53.2 %copy-start.20 = (bf16[1664,1024]{0,1:T(8,128)(2,1)S(1)}, bf16[1664,1024]{0,1:T(8,128)(2,1)}, u32[]{:S(2)}) copy-start(bf16[1664,1024]{0,1:T(8,128)(2,1)} %all-gather.11.cloned.1.call-done) | copy-start | bytes 10223620
  965.5 287.2 %reduce-scatter.12.cloned.1.call-start = ((), (), s32[]{:S(2)}) async-start(), calls=%async_computation.19 | async-start | bytes 4325376 | tf_op jit(solution)/shard_map/reduce_scatter | solution.py:272
  972.8 425.2 %reduce-scatter.14.cloned.1.call-start = ((), (), s32[]{:S(2)}) async-start(), calls=%async_computation.20 | async-start | bytes 4325376 | tf_op jit(solution)/shard_map/reduce_scatter | solution.py:275
  980.5 562.0 %reduce-scatter.16.cloned.1.call-start = ((), (), s32[]{:S(2)}) async-start(), calls=%async_computation.21 | async-start | bytes 4325376 | tf_op jit(solution)/shard_map/reduce_scatter | solution.py:278
  988.1 699.4 %reduce-scatter.18.cloned.1.call-start = ((), (), s32[]{:S(2)}) async-start(), calls=%async_computation.22 | async-start | bytes 4325376 | tf_op jit(solution)/shard_map/reduce_scatter | solution.py:281
  996.2 847.1 %reduce-scatter.10.cloned.1.call-start = ((), (), s32[]{:S(2)}) async-start(), calls=%async_computation.18 | async-start | bytes 7028736 | tf_op jit(solution)/shard_map/reduce_scatter | solution.py:269
  1004.2 1090.7 %reduce-scatter.20.cloned.1.call-start = ((), (), s32[]{:S(2)}) async-start(), calls=%async_computation.23 | async-start | bytes 11894784 | tf_op jit(solution)/shard_map/reduce_scatter | solution.py:194
  1017.9 1327.8 %reduce-scatter.22.cloned.1.call-start = ((), (), s32[]{:S(2)}) async-start(), calls=%async_computation.24 | async-start | bytes 11894784 | tf_op jit(solution)/shard_map/reduce_scatter | solution.py:197
  1031.9 1565.0 %reduce-scatter.24.cloned.1.call-start = ((), (), s32[]{:S(2)}) async-start(), calls=%async_computation.25 | async-start | bytes 11894784 | tf_op jit(solution)/shard_map/reduce_scatter | solution.py:200
  (31 other events, 90.3 us)
Sparse Core Ops, SparseCore 0:
  11.0 59.7 all-gather.26
  73.7 58.9 all-gather.10
  135.7 62.8 all-gather.16
  201.4 55.3 all-gather.14
  259.6 55.2 all-gather.12
  317.7 55.2 all-gather.18
  375.9 66.1 all-gather.20
  445.0 65.9 all-gather.22
  513.9 65.9 all-gather.24
  965.6 139.5 all-reduce.12
  1108.1 144.5 reduce-scatter.11
  1255.4 142.4 reduce-scatter.13
  1400.8 141.7 reduce-scatter.15
  1545.2 142.2 reduce-scatter.17
  1690.2 152.9 reduce-scatter.9
  1846.0 248.9 reduce-scatter.19
  2097.7 247.9 reduce-scatter.21
  2348.4 248.4 reduce-scatter.23
where the time goes:
time: 2610 us; the launch traced here: 2600 us
  waiting for transfers between devices  1730 us (66%)
  matrix products  539 us (21%)
  blocking collectives  134 us (5%)
  local copies, waits for them, and re-layouts  124 us (5%)
  other arithmetic  59.7 us (2%)
    reduce_scatter x1, waiting for transfers between devices, shards(): lax.psum_scatter(left_contract(normal_mid, grad_gate), ('row', 'col'), sc...  252 us
    reduce_scatter x1, waiting for transfers between devices, shards(): lax.psum_scatter(grad_down, ('row', 'col'), scatter_dimension=1, tiled=True)  251 us
    reduce_scatter x1, waiting for transfers between devices, shards(): lax.psum_scatter(left_contract(normal_mid, grad_upward), ('row', 'col'),...  251 us
    dot_general x57, matrix products, right_contract(): lax.dot_general(left, right, (((1,), (1,)), ((), ())), preferred_element_...  191 us
    dot_general x41, matrix products, matmul(): return jnp.dot(left, right, preferred_element_type=jnp.float32)  183 us
    dot_general x41, matrix products, left_contract(): lax.dot_general(left, right, (((0,), (0,)), ((), ())), preferred_element_...  165 us
    reduce_scatter x1, waiting for transfers between devices, shards(): lax.psum_scatter(grad_proj, ('row', 'col'), scatter_dimension=1, tiled=True)  156 us
    reduce_scatter x1, waiting for transfers between devices, shards(): lax.psum_scatter(left_contract(normal_in, grad_keys), ('row', 'col'), sca...  145 us
  transfers between devices with their start and end apart: 19, of which 15 were waited for; matrix products, arithmetic and copies ran while one was open for 14% of the time, Pallas kernels for 0%

commit v1 on v0

--- a/solution.py
+++ b/solution.py
@@ -9,6 +9,18 @@
 PATCH_SLOTS = 1024
 TEXT = 128
 ROW = 1152
+
+
+def gather_by_bits(shard, axis, dim):
+    ways, here, step = (lax.axis_size(axis), lax.axis_index(axis), shard.shape[dim])
+    line, have = (shard, 1)
+    while have < ways:
+        line = jnp.concatenate(
+            [line, lax.ppermute(line, axis, [(d, (d - have) % ways) for d in range(ways)])],
+            axis=dim,
+        )
+        have = 2 * have
+    return jnp.roll(line, here * step, axis=dim)
 
 
 def normed(values, gain):
@@ -130,7 +142,7 @@
     ) = (
         lax.all_gather(conv_weight, ("row", "col"), axis=1, tiled=True),
         lax.all_gather(conv_bias, ("row", "col"), axis=0, tiled=True),
-        lax.all_gather(proj_weight, ("row", "col"), axis=1, tiled=True),
+        gather_by_bits(proj_weight, ("row", "col"), 1),
         lax.all_gather(proj_bias, ("row", "col"), axis=0, tiled=True),
         lax.all_gather(first_gain, ("row", "col"), axis=0, tiled=True),
         lax.all_gather(query_weight, ("row", "col"), axis=0, tiled=True),

time: 2610 us -> 2570 us (0.985)
  waiting for transfers between devices: 1730 us -> 1670 us
    all_gather x1, waiting for transfers between devices: 54.7 us -> 0.02 us  [shards(): lax.all_gather(proj_weight, ('row', 'col'), axis=1, tiled=True)]
    all_to_all x1 -> x0, blocking collectives: 53 us -> none  [shards(): lax.all_to_all(grad_arrived, ('row', 'col'), split_axis=0, concat_axis=0,...]
    all_to_all x0 -> x1, waiting for transfers between devices: none -> 49.9 us  [shards(): lax.all_to_all(grad_arrived, ('row', 'col'), split_axis=0, concat_axis=0,...]
    all_gather x1, waiting for transfers between devices: 45.2 us -> 0.02 us  [shards(): lax.all_gather(query_weight, ('row', 'col'), axis=0, tiled=True)]
    ppermute x0 -> x5, waiting for transfers between devices: none -> 42.3 us  [gather_by_bits(): lax.ppermute(line, axis, [(d, (d - have) % ways) for d in range(ways)])]
    unnamed x2, blocking collectives: 81.3 us -> 111 us
  transfers between devices with their start and end apart: 19 -> 25, of which waited for: 15 -> 15; matrix products, arithmetic and copies ran while one was open for 14% -> 27% of each run, Pallas kernels for 0% -> 0%
where the time goes in v1:
time: 2570 us; the launch traced here: 2560 us
  waiting for transfers between devices  1670 us (65%)
  matrix products  536 us (21%)
  local copies, waits for them, and re-layouts  141 us (5%)
  blocking collectives  111 us (4%)
  other arithmetic  64.8 us (3%)
    reduce_scatter x1, waiting for transfers between devices, shards(): lax.psum_scatter(left_contract(normal_mid, grad_gate), ('row', 'col'), sc...  252 us
    reduce_scatter x1, waiting for transfers between devices, shards(): lax.psum_scatter(grad_down, ('row', 'col'), scatter_dimension=1, tiled=True)  251 us
    reduce_scatter x1, waiting for transfers between devices, shards(): lax.psum_scatter(left_contract(normal_mid, grad_upward), ('row', 'col'),...  250 us
    dot_general x57, matrix products, right_contract(): lax.dot_general(left, right, (((1,), (1,)), ((), ())), preferred_element_...  193 us
    dot_general x41, matrix products, matmul(): return jnp.dot(left, right, preferred_element_type=jnp.float32)  178 us
    dot_general x41, matrix products, left_contract(): lax.dot_general(left, right, (((0,), (0,)), ((), ())), preferred_element_...  165 us
    reduce_scatter x1, waiting for transfers between devices, shards(): lax.psum_scatter(grad_proj, ('row', 'col'), scatter_dimension=1, tiled=True)  155 us
    reduce_scatter x1, waiting for transfers between devices, shards(): lax.psum_scatter(left_contract(normal_in, grad_values), ('row', 'col'), s...  145 us
  transfers between devices with their start and end apart: 25, of which 15 were waited for; matrix products, arithmetic and copies ran while one was open for 27% of the time, Pallas kernels for 0%

profile of v1, /device:TPU:0, one launch (start us, length us, event | category | flops | bytes accessed | tf_op | source)
XLA Modules:
  0.0 2560.2 jit_solution(16019986434787524089)
XLA Ops:
  31.1 22.8 collective-permute-done.2
  61.6 10.1 collective-permute-done.3
  77.0 73.1 %all-reduce.10 = (bf16[1024]{0:T(1024)(128)(2,1)}, bf16[1664]{0:T(1024)(128)(2,1)}, bf16[1024]{0:T(1024)(128)(2,1)}, bf16[1024]{0:T(1024)(128)(2,1)}) all-reduce(bf16[1024]{0:T(1024)(128)(2,1)} %copy-done.20, bf16[1664]{0:T(1024)(128)(2,1)S(1)} %dynamic-update-slice, ...), channel_id=1, replica_groups=mesh['row'=4,'col'=8] {'row','col'}, use_global_device_ids=true, to_apply=%add.1 | all-reduce | flops 4736 | bytes 18944
  182.3 50.9 %all-to-all-done = bf16[32,32,1024]{2,1,0:T(8,128)(2,1)S(1)} async-done(((bf16[32,32,1024]{2,1,0:T(8,128)(2,1)}), bf16[32,32,1024]{2,1,0:T(8,128)(2,1)S(1)}, u32[]{:S(2)}, u32[]{:S(2)}) %all-to-all-start) | async-done | bytes 2097184 | tf_op jit(solution)/shard_map/all_to_all | solution.py:162
  236.3 21.4 gather_fusion
  304.3 152.1 %while.48 = (s32[]{:T(128)}, bf16[16,1152,64]{1,2,0:T(8,128)(2,1)}, f32[16,1152]{1,0:T(8,128)S(1)}, bf16[16,1152,64]{2,1,0:T(8,128)(2,1)}, bf16[16,1152,64]{2,1,...) while((s32[]{:T(128)}, bf16[16,1152,64]{1,2,0:T(8,128)(2,1)}, ...), condition=%wide.region_4.5_spmd.clone, body=%wide.region_1.4_spmd.clone.sunk | while | flops 351681408 | bytes 38412412 | solution.py:75
  466.4 13.2 fusion.94
  479.6 13.0 fusion.95
  492.7 40.6 %all-gather.23.cloned.1.call-done = bf16[2816,1024]{0,1:T(8,128)(2,1)} async-done(((bf16[2816,32]{0,1:T(8,128)(2,1)}), bf16[2816,1024]{0,1:T(8,128)(2,1)}) %all-gather.23.cloned.1.call-update) | async-done | bytes 5767184 | tf_op jit(solution)/shard_map/all_gather | solution.py:157
  533.3 25.5 multiply_convert_fusion.1
  558.9 13.4 fusion.96
  572.3 11.6 multiply_reduce_fusion.1
  602.9 209.3 %while.49 = (s32[]{:T(128)}, bf16[16,1152,64]{1,2,0:T(8,128)(2,1)}, bf16[16,1152,64]{1,2,0:T(8,128)(2,1)}, bf16[16,1152,64]{1,2,0:T(8,128)(2,1)}, bf16[16,1152,6...) while((s32[]{:T(128)}, bf16[16,1152,64]{1,2,0:T(8,128)(2,1)}, ...), condition=%wide.region_9.10_spmd.clone, body=%wide.region_7.9_spmd.clone.sunk | while | flops 862763904 | bytes 42810480 | solution.py:98
  834.9 17.7 scatter_custom_fusion
  860.6 49.9 %all-to-all-done.1 = bf16[32,32,1024]{2,1,0:T(8,128)(2,1)S(1)} async-done(((bf16[32,32,1024]{2,1,0:T(8,128)(2,1)}), bf16[32,32,1024]{2,1,0:T(8,128)(2,1)S(1)}, u32[]{:S(2)}, u32[]{:S(2)}) %all-to-all-start.1) | async-done | bytes 2097184 | tf_op jit(solution)/shard_map/all_to_all | solution.py:269
  922.8 7.9 fusion.73
  931.0 7.5 fusion.84
  938.6 7.4 fusion.86
  953.5 8.0 fusion.98
  961.5 13.6 fusion.100
  975.6 13.6 fusion.99
  989.2 13.6 fusion.101
  1002.9 13.3 add_convert_fusion.1
  1020.9 38.0 %all-reduce.9 = (f32[1664]{0:T(1024)S(1)}, f32[1024]{0:T(1024)S(1)}, f32[1024]{0:T(1024)S(1)}, f32[1024]{0:T(1024)S(1)}) all-reduce(f32[1664]{0:T(1024)S(1)} %get-tuple-element.317, f32[1024]{0:T(1024)S(1)} %convert_reduce_fusion.1, f32[1024]{0:T(1024)S(1)} %get-tuple-element.250, ...), channel_id=3, replica_groups=mesh['row'=4,'col'=8] {'row','col'}, use_global_device_ids=true, to_apply=%region_14.15.clone | all-reduce | flops 4736 | bytes 37888
  1070.4 139.7 %reduce-scatter.18.cloned.1.call-done = f32[1024,32]{0,1:T(8,128)} async-done(((f32[1024,1024]{0,1:T(8,128)}), f32[1024,32]{0,1:T(8,128)}) %reduce-scatter.18.cloned.1.call-update) | async-done | bytes 131088 | tf_op jit(solution)/shard_map/reduce_scatter | solution.py:293
  1210.1 145.1 %reduce-scatter.16.cloned.1.call-done = f32[32,1024]{1,0:T(8,128)} async-done(((f32[1024,1024]{1,0:T(8,128)}), f32[32,1024]{1,0:T(8,128)}) %reduce-scatter.16.cloned.1.call-update) | async-done | bytes 131088 | tf_op jit(solution)/shard_map/reduce_scatter | solution.py:290
  1355.2 145.0 %reduce-scatter.14.cloned.1.call-done = f32[32,1024]{1,0:T(8,128)} async-done(((f32[1024,1024]{1,0:T(8,128)}), f32[32,1024]{1,0:T(8,128)}) %reduce-scatter.14.cloned.1.call-update) | async-done | bytes 131088 | tf_op jit(solution)/shard_map/reduce_scatter | solution.py:287
  1500.2 144.4 %reduce-scatter.12.cloned.1.call-done = f32[32,1024]{1,0:T(8,128)} async-done(((f32[1024,1024]{1,0:T(8,128)}), f32[32,1024]{1,0:T(8,128)}) %reduce-scatter.12.cloned.1.call-update) | async-done | bytes 131088 | tf_op jit(solution)/shard_map/reduce_scatter | solution.py:284
  1644.5 155.4 %reduce-scatter.10.cloned.1.call-done = f32[1664,32]{0,1:T(8,128)} async-done(((f32[1664,1024]{0,1:T(8,128)}), f32[1664,32]{0,1:T(8,128)}) %reduce-scatter.10.cloned.1.call-update) | async-done | bytes 213008 | tf_op jit(solution)/shard_map/reduce_scatter | solution.py:281
  1799.9 249.8 %reduce-scatter.22.cloned.1.call-done = f32[32,2816]{1,0:T(8,128)} async-done(((f32[1024,2816]{1,0:T(8,128)}), f32[32,2816]{1,0:T(8,128)}) %reduce-scatter.22.cloned.1.call-update) | async-done | bytes 360464 | tf_op jit(solution)/shard_map/reduce_scatter | solution.py:209
  2049.8 252.1 %reduce-scatter.20.cloned.1.call-done = f32[32,2816]{1,0:T(8,128)} async-done(((f32[1024,2816]{1,0:T(8,128)}), f32[32,2816]{1,0:T(8,128)}) %reduce-scatter.20.cloned.1.call-update) | async-done | bytes 360464 | tf_op jit(solution)/shard_map/reduce_scatter | solution.py:206
  2301.9 251.2 %reduce-scatter.24.cloned.1.call-done = f32[2816,32]{0,1:T(8,128)} async-done(((f32[2816,1024]{0,1:T(8,128)}), f32[2816,32]{0,1:T(8,128)}) %reduce-scatter.24.cloned.1.call-update) | async-done | bytes 360464 | tf_op jit(solution)/shard_map/reduce_scatter | solution.py:212
  (453 shorter events, 574.8 us)
Async XLA Ops:
  7.2 155.9 %copy-start = (bf16[32,32,588]{2,1,0:T(8,128)(2,1)S(1)}, bf16[32,32,588]{2,1,0:T(8,128)(2,1)}, u32[]{:S(2)}) copy-start(bf16[32,32,588]{2,1,0:T(8,128)(2,1)} %param.22) | copy-start | bytes 3612676
  7.2 65.9 %copy-start.34 = (bf16[32]{0:T(256)(128)(2,1)S(1)}, bf16[32]{0:T(256)(128)(2,1)}, u32[]{:S(2)}) copy-start(bf16[32]{0:T(256)(128)(2,1)} %param.30) | copy-start | bytes 196
  7.2 153.1 %all-gather.27.cloned.1.call-start = ((), (), s32[]{:S(2)}) async-start(), calls=%async_computation.26 | async-start | bytes 2365440 | tf_op jit(solution)/shard_map/all_gather | solution.py:143
  7.9 256.9 %all-gather.15.cloned.1.call-start = ((), (), s32[]{:S(2)}) async-start(), calls=%async_computation.12 | async-start | bytes 2162688 | tf_op jit(solution)/shard_map/all_gather | solution.py:150
  8.7 268.6 %all-gather.13.cloned.1.call-start = ((), (), s32[]{:S(2)}) async-start(), calls=%async_computation.11 | async-start | bytes 2162688 | tf_op jit(solution)/shard_map/all_gather | solution.py:149
  9.4 280.8 %all-gather.11.cloned.1.call-start = ((), (), s32[]{:S(2)}) async-start(), calls=%async_computation.10 | async-start | bytes 2162688 | tf_op jit(solution)/shard_map/all_gather | solution.py:148
  10.0 446.4 %all-gather.17.cloned.1.call-start = ((), (), s32[]{:S(2)}) async-start(), calls=%async_computation.13 | async-start | bytes 2162688 | tf_op jit(solution)/shard_map/all_gather | solution.py:151
  10.6 455.9 %all-gather.19.cloned.1.call-start = ((), (), s32[]{:S(2)}) async-start(), calls=%async_computation.14 | async-start | bytes 5947392 | tf_op jit(solution)/shard_map/all_gather | solution.py:155
  11.2 468.5 %all-gather.21.cloned.1.call-start = ((), (), s32[]{:S(2)}) async-start(), calls=%async_computation.15 | async-start | bytes 5947392 | tf_op jit(solution)/shard_map/all_gather | solution.py:156
  11.9 521.4 %all-gather.23.cloned.1.call-start = ((), (), s32[]{:S(2)}) async-start(), calls=%async_computation.16 | async-start | bytes 5947392 | tf_op jit(solution)/shard_map/all_gather | solution.py:157
  12.7 9.2 collective-permute-start
  21.8 51.3 %copy-start.10 = (bf16[1664,32]{0,1:T(8,128)(2,1)}, bf16[1664,32]{0,1:T(8,128)(2,1)S(1)}, u32[]{:S(2)}) copy-start(bf16[1664,32]{0,1:T(8,128)(2,1)S(1)} %collective-permute-done) | copy-start | bytes 319492
  22.8 7.2 collective-permute-start.1
  30.0 43.1 %copy-start.9 = (bf16[1664,64]{0,1:T(8,128)(2,1)}, bf16[1664,64]{0,1:T(8,128)(2,1)S(1)}, u32[]{:S(2)}) copy-start(bf16[1664,64]{0,1:T(8,128)(2,1)S(1)} %collective-permute-done.1) | copy-start | bytes 638980
  31.0 22.9 collective-permute-start.2
  54.9 98.5 %copy-start.6 = (bf16[1664,32]{0,1:T(8,128)(2,1)S(1)}, bf16[1664,32]{0,1:T(8,128)(2,1)}, u32[]{:S(2)}) copy-start(bf16[1664,32]{0,1:T(8,128)(2,1)} %param.29) | copy-start | bytes 319492
  54.9 16.8 collective-permute-start.3
  73.1 79.0 %collective-permute-start.4 = (bf16[1664,512]{0,1:T(8,128)(2,1)}, bf16[1664,512]{0,1:T(8,128)(2,1)S(1)}, u32[]{:S(2)}, u32[]{:S(2)}) collective-permute-start(bf16[1664,512]{0,1:T(8,128)(2,1)} %get-tuple-element.301), channel_id=1, source_target_pairs={{0,16},{1,17},{2,18},{3,19},{4,20},{5,21},{6,22},{7,23},{8,24},{9,... | collective-permute-start | bytes 5111816 | tf_op jit(solution)/shard_map/ppermute | solution.py:19
  172.1 61.2 %all-to-all-start = ((bf16[32,32,1024]{2,1,0:T(8,128)(2,1)}), bf16[32,32,1024]{2,1,0:T(8,128)(2,1)S(1)}, u32[]{:S(2)}, u32[]{:S(2)}) async-start(bf16[32,32,1024]{2,1,0:T(8,128)(2,1)} %bitcast.190), calls=%async_computation | async-start | bytes 4194304 | tf_op jit(solution)/shard_map/all_to_all | solution.py:162
  176.3 684.3 %all-gather.25.cloned.1.call-start = ((), (), s32[]{:S(2)}) async-start(), calls=%async_computation.17 | async-start | bytes 3514368 | tf_op jit(solution)/shard_map/all_gather | solution.py:232
  177.1 113.1 %copy-start.18 = (f32[1024]{0:T(1024)}, f32[1024]{0:T(1024)S(1)}, u32[]{:S(2)}) copy-start(f32[1024]{0:T(1024)S(1)} %convert_element_type.168) | copy-start | bytes 12292
  602.9 209.3 %copy-start.31 = (bf16[1024,1024]{1,0:T(8,128)(2,1)S(1)}, bf16[1024,1024]{1,0:T(8,128)(2,1)}, u32[]{:S(2)}) copy-start(bf16[1024,1024]{1,0:T(8,128)(2,1)} %all-gather.13.cloned.1.call-done) | copy-start | bytes 6291460
  857.2 53.2 %all-to-all-start.1 = ((bf16[32,32,1024]{2,1,0:T(8,128)(2,1)}), bf16[32,32,1024]{2,1,0:T(8,128)(2,1)S(1)}, u32[]{:S(2)}, u32[]{:S(2)}) async-start(bf16[32,32,1024]{2,1,0:T(8,128)(2,1)} %bitcast.177), calls=%async_computation.1 | async-start | bytes 4194304 | tf_op jit(solution)/shard_map/all_to_all | solution.py:269
  860.5 207.9 %all-reduce.13.cloned.1.call-start = ((), (), s32[]{:S(2)}) async-start(), calls=%async_computation.27 | async-start | bytes 7880704
  922.8 287.3 %reduce-scatter.18.cloned.1.call-start = ((), (), s32[]{:S(2)}) async-start(), calls=%async_computation.22 | async-start | bytes 4325376 | tf_op jit(solution)/shard_map/reduce_scatter | solution.py:293
  930.8 424.4 %reduce-scatter.16.cloned.1.call-start = ((), (), s32[]{:S(2)}) async-start(), calls=%async_computation.21 | async-start | bytes 4325376 | tf_op jit(solution)/shard_map/reduce_scatter | solution.py:290
  938.5 561.6 %reduce-scatter.14.cloned.1.call-start = ((), (), s32[]{:S(2)}) async-start(), calls=%async_computation.20 | async-start | bytes 4325376 | tf_op jit(solution)/shard_map/reduce_scatter | solution.py:287
  946.0 698.5 %reduce-scatter.12.cloned.1.call-start = ((), (), s32[]{:S(2)}) async-start(), calls=%async_computation.19 | async-start | bytes 4325376 | tf_op jit(solution)/shard_map/reduce_scatter | solution.py:284
  953.4 846.5 %reduce-scatter.10.cloned.1.call-start = ((), (), s32[]{:S(2)}) async-start(), calls=%async_computation.18 | async-start | bytes 7028736 | tf_op jit(solution)/shard_map/reduce_scatter | solution.py:281
  961.5 1088.3 %reduce-scatter.22.cloned.1.call-start = ((), (), s32[]{:S(2)}) async-start(), calls=%async_computation.24 | async-start | bytes 11894784 | tf_op jit(solution)/shard_map/reduce_scatter | solution.py:209
  975.1 1326.7 %reduce-scatter.20.cloned.1.call-start = ((), (), s32[]{:S(2)}) async-start(), calls=%async_computation.23 | async-start | bytes 11894784 | tf_op jit(solution)/shard_map/reduce_scatter | solution.py:206
  989.2 1563.9 %reduce-scatter.24.cloned.1.call-start = ((), (), s32[]{:S(2)}) async-start(), calls=%async_computation.25 | async-start | bytes 11894784 | tf_op jit(solution)/shard_map/reduce_scatter | solution.py:212
  (48 other events, 240.8 us)
Sparse Core Ops, SparseCore 0:
  11.0 70.9 all-gather.26
  85.0 56.3 all-gather.14
  144.3 66.1 all-gather.12
  213.3 55.0 all-gather.10
  271.3 55.2 all-gather.16
  329.3 66.1 all-gather.18
  398.4 65.9 all-gather.20
  467.3 65.9 all-gather.22
  536.2 58.7 all-gather.24
  922.9 140.1 all-reduce.12
  1066.0 144.0 reduce-scatter.17
  1212.8 142.3 reduce-scatter.15
  1358.0 142.0 reduce-scatter.13
  1502.9 141.6 reduce-scatter.11
  1647.3 152.6 reduce-scatter.9
  1802.7 247.0 reduce-scatter.21
  2052.5 249.3 reduce-scatter.19
  2304.6 248.4 reduce-scatter.23
